TPU v7x, 256 devices: a whole 4x4x8 slice. The times are simulated.
256 devices in a mesh: tile: 32 (over z_hi, x, core), lev: 4 (over y), sec: 2 (over z_lo).
Axes of the slice: x: 4, y: 4, z: 8 (z_hi: 4, z_lo: 2; z = z_hi * 2 + z_lo), core: 2. Of those that a mesh axis runs over, the one named last changes fastest.
Arguments:
- forcing: float32 [8, 72, 1280, 384], P('sec', 'lev', 'tile'), may hold values from -6 to 6
- courant_x: bfloat16 [72, 1280, 384], P('lev', 'tile'), may hold values from -0.44921875 to 0.44921875
- courant_y: bfloat16 [72, 1280, 384], P('lev', 'tile'), may hold values from -0.44921875 to 0.44921875
- mass_flux: bfloat16 [72, 1280, 384], P('lev', 'tile'), may hold values from 0 to 0.59765625
- limiter_code: int32 [72, 1280, 384], P('lev', 'tile'), may hold values from 0 to 15
- seam_code: int32 [32, 2], replicated, may hold values from 0 to 1
- level_weight: float32 [72], P('lev'), may hold values from 0.02 to 0.5
- sector_share: float32 [8, 1280, 384], P('sec', 'tile'), may hold values from 0.1 to 1
- flux_cell: int32 [1024, 480], P('tile'), may hold values from 0 to 15359
Outputs:
- adjoint_start: float32 [8, 72, 1280, 384], P('sec', 'lev', 'tile')
- flux_sensitivity: float32 [491520], P('tile')
All inputs are finite; a program needn't handle non-finite values.
Results may differ from a plain program's by a relative error of at most 0.0003.
Values sent between devices are 32-bit elements; how exact they have to be, the bound alone decides.
A program may use at most 128 MiB of HBM per device.

v0:
```python
import jax
import jax.numpy as jnp
from jax import lax
from jax.sharding import PartitionSpec as P

FL_DEV = 15360


def from_behind(value, axis, steps):
    count = lax.axis_size(axis)
    initial, last = (max(0, -steps), min(count, count - steps))
    return lax.ppermute(value, axis, [(source, source + steps) for source in range(initial, last)])


def extended_2(value, sides, width):
    for axis, dim in sides:
        devices, length = (lax.axis_size(axis), value.shape[dim])
        up = [(i, (i + 1) % devices) for i in range(devices)]
        down = [(j, i) for i, j in up]
        last = lax.slice_in_dim(value, length - width, length, axis=dim)
        initial = lax.slice_in_dim(value, 0, width, axis=dim)
        before = lax.ppermute(last, axis, up)
        after = lax.ppermute(initial, axis, down)
        value = jnp.concatenate([before, value, after], axis=dim)
    return value


def coefficients(courant, codes, bit):
    value = courant.astype(jnp.float32)
    limited = jnp.bitwise_and(jnp.right_shift(codes, bit), 1).astype(jnp.float32)
    spread = 0.5 * jnp.abs(value) * (1.0 - jnp.abs(value))
    ahead = jnp.maximum(value, 0.0) - limited * spread
    behind = jnp.minimum(value, 0.0) + limited * spread
    return (ahead, behind)


def flipped(rim, flag):
    return jnp.where(flag, rim[..., ::-1], rim)


def vertical(adjoint, mixing, at_top):
    above = from_behind(adjoint[:, :1], "lev", -1)
    above = jnp.where(at_top, adjoint[:, -1:], above)
    upper = jnp.concatenate([adjoint[:, 1:], above], axis=1)
    return adjoint + mixing * (upper - adjoint)


def sweep_second(adjoint, courant, codes, bit):
    ahead, behind = coefficients(courant, codes, bit)
    following = jnp.concatenate([adjoint[..., 1:], adjoint[..., -1:]], axis=-1)
    previous = jnp.concatenate([adjoint[..., :1], adjoint[..., :-1]], axis=-1)
    return adjoint + ahead * (following - adjoint) + behind * (adjoint - previous)


def sweep_first(adjoint, courant, codes, bit, flip_left, flip_right):
    ahead, behind = coefficients(courant, codes, bit)
    extended = extended_2(adjoint, (("tile", 2),), 1)
    left_rim = flipped(extended[:, :, :1], flip_left)
    right_rim = flipped(extended[:, :, -1:], flip_right)
    following = jnp.concatenate([adjoint[:, :, 1:], right_rim], axis=2)
    previous = jnp.concatenate([left_rim, adjoint[:, :, :-1]], axis=2)
    return adjoint + ahead * (following - adjoint) + behind * (adjoint - previous)


def shards(
    forcing,
    courant_x,
    courant_y,
    mass_flux,
    limiter_code,
    seam_code,
    level_weight,
    sector_share,
    flux_cell,
):
    mixing = mass_flux.astype(jnp.float32)
    at_top = lax.axis_index("lev") == lax.axis_size("lev") - 1
    tile_count = lax.axis_size("tile")
    tile_rank = lax.axis_index("tile")
    place = jnp.remainder(tile_rank + tile_count, tile_count)
    seams_here = lax.dynamic_index_in_dim(seam_code, place, 0, keepdims=False) == 1
    adjoint = forcing
    for turn_index in (1, 0):
        adjoint = vertical(adjoint, mixing, at_top)
        adjoint = sweep_second(adjoint, courant_y, limiter_code, 2 * turn_index + 1)
        adjoint = sweep_first(
            adjoint, courant_x, limiter_code, 2 * turn_index, seams_here[0], seams_here[1]
        )
    partial_value = jnp.einsum(
        "sxy,l,slxy->xy", sector_share, level_weight, adjoint, precision=lax.Precision.HIGHEST
    )
    columns = partial_value.reshape(tile_count, -1)
    totals = lax.psum(columns, ("lev", "sec"))
    received = lax.all_to_all(totals, "tile", split_axis=0, concat_axis=0, tiled=True)
    flux_sensitivity = jax.ops.segment_sum(
        received.reshape(-1), flux_cell.reshape(-1), num_segments=FL_DEV
    )
    return (adjoint, flux_sensitivity)


def solution(mesh):
    placed = (
        P("sec", "lev", "tile", None),
        P("lev", "tile", None),
        P("lev", "tile", None),
        P("lev", "tile", None),
        P("lev", "tile", None),
        P(),
        P("lev"),
        P("sec", "tile", None),
        P("tile", None),
    )
    return jax.shard_map(
        shards,
        mesh=mesh,
        in_specs=placed,
        out_specs=(P("sec", "lev", "tile", None), P("tile")),
        check_vma=False,
    )
```

profile of v0, /device:TPU:1, one launch (start us, length us, event | category | flops | bytes accessed | tf_op | source)
XLA Modules:
  0.0 220.0 jit_solution(4765529639356526114)
XLA Ops:
  1.8 1.4 collective-permute-start
  3.2 5.8 %fusion.28 = (f32[18,40,384]{2,1,0:T(8,128)}, f32[18,40,384]{2,1,0:T(8,128)}, f32[18,40,384]{2,1,0:T(8,128)}, f32[18,40,384]{2,1,0:T(8,128)}, f32[18,40,384]{2,1...) fusion(bf16[18,40,384]{2,1,0:T(8,128)(2,1)} %param.10, ...), kind=kLoop, calls=%fused_computation.45 | loop fusion | flops 10506240 | bytes 11059200 | tf_op jit(solution)/shard_map/sub | solution.py:32
  9.0 2.3 %slice.76 = f32[4,17,40,384]{3,2,1,0:T(8,128)} slice(f32[4,18,40,384]{3,2,1,0:T(8,128)S(1)} %bitcast.18), slice={[0:4], [1:18], [0:40], [0:384]} | slice | bytes 8355840 | tf_op jit(solution)/shard_map/slice | solution.py:44
  13.0 4.2 %fusion.3 = f32[4,18,40,384]{3,2,1,0:T(8,128)S(1)} fusion(f32[4,18,40,384]{3,2,1,0:T(8,128)} %param.9, f32[4,1,40,384]{3,2,1,0:T(8,128)S(1)} %slice_select_fusion.1, f32[4,17,40,384]{3,2,1,0:T(8,128)} %slice.76, f32[18,40,384]{2,1,0:T(8,128)S(1)} %convert_element_type.23), kind=kLoop, calls=%fused_computation.5 | loop fusion | flops 4423680 | bytes 14376960 | tf_op jit(solution)/shard_map/add | solution.py:45
  17.2 1.6 fusion.46
  18.8 1.4 fusion.47
  20.2 3.7 %fusion.6 = f32[4,18,40,384]{3,2,1,0:T(8,128)S(1)} fusion(f32[4,18,40,384]{3,2,1,0:T(8,128)S(1)} %fusion.3, f32[4,18,40,1]{3,2,1,0:T(8,128)} %get-tuple-element.17, f32[4,18,40,383]{3,2,1,0:T(8,128)S(1)} %get-tuple-element.19, f32[4,18,40,383]{3,2,1,0:T(8,128)S(1)} %get-tuple-element.18, f32[4,18,40,1]{3,2,1,0:T(8,128)S(1)} %get-tuple-element.16, ...), kind=kLoop, calls=%fused_computation.9 | loop fusion | flops 8847360 | bytes 19906560 | tf_op jit(solution)/shard_map/add | solution.py:52
  24.1 3.3 %collective-permute-start.1 = (f32[4,18,1,384]{3,1,2,0:T(8,128)S(1)}, f32[4,18,1,384]{3,1,2,0:T(8,128)S(1)}, u32[]{:S(2)}, u32[]{:S(2)}) collective-permute-start(f32[4,18,1,384]{3,1,2,0:T(8,128)S(1)} %copy.26), channel_id=1, source_target_pairs={{8,0},{16,8},{24,16},{32,24},{40,32},{48,40},{56,48},{64,56},{72,6... | collective-permute-start | bytes 331784 | tf_op jit(solution)/shard_map/ppermute | solution.py:23
  27.5 4.1 %fusion.45 = (f32[4,18,39,384]{3,2,1,0:T(8,128)}, f32[4,18,39,384]{3,2,1,0:T(8,128)}) fusion(f32[4,18,40,384]{3,2,1,0:T(8,128)S(1)} %fusion.6), kind=kLoop, calls=%fused_computation.74 | loop fusion | bytes 17252352 | tf_op jit(solution)/shard_map/slice | solution.py:61
  32.4 2.2 collective-permute-done.2
  37.0 5.9 %fusion.10 = f32[4,18,40,384]{3,2,1,0:T(8,128)S(1)} fusion(f32[4,18,40,384]{3,2,1,0:T(8,128)} %copy-done.2, f32[4,18,1,384]{3,2,1,0:T(1,128)S(1)} %broadcast_select_fusion.3, f32[4,18,39,384]{3,2,1,0:T(8,128)} %get-tuple-element.15, f32[4,18,39,384]{3,2,1,0:T(8,128)} %get-tuple-element.14, f32[4,18,1,384]{3,2,1,0:T(1,128)S(1)} %broadcast_select_fusion.1, ...), kind=kLoop, calls=%fused_computation.15 | loop fusion | flops 8847360 | bytes 19906560 | tf_op jit(solution)/shard_map/add | solution.py:62
  42.9 1.5 collective-permute-start.3
  44.7 5.8 %collective-permute-done.3 = f32[4,1,40,384]{3,2,1,0:T(8,128)S(1)} collective-permute-done((f32[4,1,40,384]{3,2,1,0:T(8,128)S(1)}, f32[4,1,40,384]{3,2,1,0:T(8,128)S(1)}, u32[]{:S(2)}, u32[]{:S(2)}) %collective-permute-start.3) | collective-permute-done | bytes 245792 | tf_op jit(solution)/shard_map/ppermute | solution.py:12
  51.7 1.4 fusion.43
  53.1 3.5 %fusion.16 = f32[4,18,40,384]{3,2,1,0:T(8,128)S(1)} fusion(f32[4,18,40,384]{3,2,1,0:T(8,128)S(1)} %fusion.13, f32[4,18,40,1]{3,2,1,0:T(8,128)S(1)} %get-tuple-element.9, f32[4,18,40,383]{3,2,1,0:T(8,128)S(1)} %get-tuple-element.11, f32[4,18,40,383]{3,2,1,0:T(8,128)S(1)} %get-tuple-element.10, f32[4,18,40,1]{3,2,1,0:T(8,128)S(1)} %get-tuple-element.8, ...), kind=kLoop, calls=%fused_computation.24 | loop fusion | flops 8847360 | bytes 19906560 | tf_op jit(solution)/shard_map/add | solution.py:52
  56.8 9.9 %collective-permute-start.4 = (f32[4,18,1,384]{3,1,2,0:T(8,128)S(1)}, f32[4,18,1,384]{3,1,2,0:T(8,128)S(1)}, u32[]{:S(2)}, u32[]{:S(2)}) collective-permute-start(f32[4,18,1,384]{3,1,2,0:T(8,128)S(1)} %copy.32), channel_id=1, source_target_pairs={{8,0},{16,8},{24,16},{32,24},{40,32},{48,40},{56,48},{64,56},{72,6... | collective-permute-start | bytes 331784 | tf_op jit(solution)/shard_map/ppermute | solution.py:23
  66.8 4.1 %fusion.41 = (f32[4,18,39,384]{3,2,1,0:T(8,128)}, f32[4,18,39,384]{3,2,1,0:T(8,128)}) fusion(f32[4,18,40,384]{3,2,1,0:T(8,128)S(1)} %fusion.16), kind=kLoop, calls=%fused_computation.70 | loop fusion | bytes 17252352 | tf_op jit(solution)/shard_map/slice | solution.py:61
  74.2 5.7 %fusion.20 = f32[4,18,40,384]{3,2,1,0:T(8,128)S(1)} fusion(f32[4,18,40,384]{3,2,1,0:T(8,128)} %copy-done.1, f32[4,18,1,384]{3,2,1,0:T(1,128)S(1)} %broadcast_select_fusion.2, f32[4,18,39,384]{3,2,1,0:T(8,128)} %get-tuple-element.7, f32[4,18,39,384]{3,2,1,0:T(8,128)} %get-tuple-element.6, f32[4,18,1,384]{3,2,1,0:T(1,128)S(1)} %broadcast_select_fusion, ...), kind=kLoop, calls=%fused_computation.30 | loop fusion | flops 8847360 | bytes 19906560 | tf_op jit(solution)/shard_map/add | solution.py:62
  79.9 2.1 copy-done.3
  82.0 4.4 %fusion = f32[1,4,40,384]{3,0,2,1:T(1,128)S(1)} fusion(f32[4,18,40,384]{3,2,1,0:T(8,128)S(1)} %fusion.20, f32[18]{0:T(128)S(1)} %copy-done), kind=kOutput, calls=%fused_computation.1 | convolution fusion | flops 13271040 | bytes 4669512 | tf_op jit(solution)/shard_map/sxy,l,slxy->xy/dot_general | solution.py:89
  86.5 27.3 %psum.7 = f32[32,1,480]{2,1,0:T(1,128)} all-reduce(f32[32,1,480]{2,1,0:T(1,128)S(1)} %all_to_all.6), channel_id=1, replica_groups=mesh['tile'=32,'lev'=4,'sec'=2] {'lev','sec'}, use_global_device_ids=true, to_apply=%region_0.1 | all-reduce | flops 15360 | bytes 122880 | tf_op jit(solution)/shard_map/psum | solution.py:93
  113.9 14.8 %all-to-all-start = ((f32[32,1,480]{2,1,0:T(1,128)}), f32[32,1,480]{2,1,0:T(1,128)S(1)}, u32[]{:S(2)}, u32[]{:S(2)}) async-start(f32[32,1,480]{2,1,0:T(1,128)} %psum.7), calls=%async_computation | async-start | bytes 131072 | tf_op jit(solution)/shard_map/all_to_all | solution.py:94
  128.8 9.9 %all-to-all-done = f32[32,1,480]{2,1,0:T(1,128)S(1)} async-done(((f32[32,1,480]{2,1,0:T(1,128)}), f32[32,1,480]{2,1,0:T(1,128)S(1)}, u32[]{:S(2)}, u32[]{:S(2)}) %all-to-all-start) | async-done | bytes 61472 | tf_op jit(solution)/shard_map/all_to_all | solution.py:94
  139.0 81.0 %scatter_custom_fusion = f32[15360]{0:T(1024)} fusion(s32[15360]{0:T(1024)S(1)} %reshape.33, f32[15360]{0:T(1024)S(1)} %reshape.35, f32[]{:T(128)} %constant.16.clone.1), kind=kCustom, calls=%fused_computation.65 | custom fusion | flops 15360 | bytes 61444 | tf_op jit(solution)/shard_map/scatter-add | solution.py:95
  (65 shorter events, 11.8 us)
Async XLA Ops:
  0.6 81.3 %copy-start = (f32[18]{0:T(128)S(1)}, f32[18]{0:T(128)}, u32[]{:S(2)}) copy-start(f32[18]{0:T(128)} %param.15) | copy-start | bytes 220
  0.6 8.3 %slice-start = ((s8[4423680]{0:T(1024)(128)(4,1)}), s8[4194304]{0:T(1024)(128)(4,1)S(1)}, s32[]{:S(2)}) async-start(s8[4423680]{0:T(1024)(128)(4,1)} %bitcast.17), calls=%async_computation.1 | async-start | bytes 8388608
  1.8 7.2 %slice-start.1 = ((s8[4423680]{0:T(1024)(128)(4,1)}), s8[229376]{0:T(1024)(128)(4,1)S(1)}, s32[]{:S(2)}) async-start(s8[4423680]{0:T(1024)(128)(4,1)} %bitcast.17), calls=%async_computation.2 | async-start | bytes 458752
  1.8 10.2 %collective-permute-start = (f32[4,1,40,384]{3,2,1,0:T(8,128)S(1)}, f32[4,1,40,384]{3,2,1,0:T(8,128)S(1)}, u32[]{:S(2)}, u32[]{:S(2)}) collective-permute-start(f32[4,1,40,384]{3,2,1,0:T(8,128)S(1)} %slice.78), channel_id=1, source_target_pairs={{2,0},{4,2},{6,4},{3,1},{5,3},{7,5},{10,8},{12,10},{14,12},{11,9},... | collective-permute-start | bytes 737288 | tf_op jit(solution)/shard_map/ppermute | solution.py:12
  9.0 2.3 %copy-start.7 = (bf16[18,40,384]{2,1,0:T(8,128)(2,1)S(1)}, bf16[18,40,384]{2,1,0:T(8,128)(2,1)}, u32[]{:S(2)}) copy-start(bf16[18,40,384]{2,1,0:T(8,128)(2,1)} %param.12) | copy-start | bytes 1658884
  9.0 2.4 %copy-start.10 = (s32[32,2]{0,1:T(2,128)S(1)}, s32[32,2]{0,1:T(2,128)}, u32[]{:S(2)}) copy-start(s32[32,2]{0,1:T(2,128)} %param.14) | copy-start | bytes 772
  23.9 7.7 %copy-start.2 = (f32[4,18,40,384]{3,2,1,0:T(8,128)}, f32[4,18,40,384]{3,2,1,0:T(8,128)S(1)}, u32[]{:S(2)}) copy-start(f32[4,18,40,384]{3,2,1,0:T(8,128)S(1)} %fusion.6) | copy-start | bytes 13271044
  24.1 7.5 %collective-permute-start.1 = (f32[4,18,1,384]{3,1,2,0:T(8,128)S(1)}, f32[4,18,1,384]{3,1,2,0:T(8,128)S(1)}, u32[]{:S(2)}, u32[]{:S(2)}) collective-permute-start(f32[4,18,1,384]{3,1,2,0:T(8,128)S(1)} %copy.26), channel_id=1, source_target_pairs={{8,0},{16,8},{24,16},{32,24},{40,32},{48,40},{56,48},{64,56},{72,6... | collective-permute-start | bytes 331784 | tf_op jit(solution)/shard_map/ppermute | solution.py:23
  27.4 9.6 %copy-start.6 = (f32[18,40,384]{2,1,0:T(8,128)S(1)}, f32[18,40,384]{2,1,0:T(8,128)}, u32[]{:S(2)}) copy-start(f32[18,40,384]{2,1,0:T(8,128)} %get-tuple-element.22) | copy-start | bytes 3317764
  27.4 7.1 %collective-permute-start.2 = (f32[4,18,1,384]{3,1,2,0:T(8,128)S(1)}, f32[4,18,1,384]{3,1,2,0:T(8,128)S(1)}, u32[]{:S(2)}, u32[]{:S(2)}) collective-permute-start(f32[4,18,1,384]{3,1,2,0:T(8,128)S(1)} %copy.29), channel_id=1, source_target_pairs={{0,8},{8,16},{16,24},{24,32},{32,40},{40,48},{48,56},{56,64},{64,7... | collective-permute-start | bytes 331784 | tf_op jit(solution)/shard_map/ppermute | solution.py:22
  42.9 7.6 %collective-permute-start.3 = (f32[4,1,40,384]{3,2,1,0:T(8,128)S(1)}, f32[4,1,40,384]{3,2,1,0:T(8,128)S(1)}, u32[]{:S(2)}, u32[]{:S(2)}) collective-permute-start(f32[4,1,40,384]{3,2,1,0:T(8,128)S(1)} %slice.110), channel_id=1, source_target_pairs={{2,0},{4,2},{6,4},{3,1},{5,3},{7,5},{10,8},{12,10},{14,12},{11,9},... | collective-permute-start | bytes 737288 | tf_op jit(solution)/shard_map/ppermute | solution.py:12
  56.6 14.3 %copy-start.1 = (f32[4,18,40,384]{3,2,1,0:T(8,128)}, f32[4,18,40,384]{3,2,1,0:T(8,128)S(1)}, u32[]{:S(2)}) copy-start(f32[4,18,40,384]{3,2,1,0:T(8,128)S(1)} %fusion.16) | copy-start | bytes 13271044
  56.8 14.1 %collective-permute-start.4 = (f32[4,18,1,384]{3,1,2,0:T(8,128)S(1)}, f32[4,18,1,384]{3,1,2,0:T(8,128)S(1)}, u32[]{:S(2)}, u32[]{:S(2)}) collective-permute-start(f32[4,18,1,384]{3,1,2,0:T(8,128)S(1)} %copy.32), channel_id=1, source_target_pairs={{8,0},{16,8},{24,16},{32,24},{40,32},{48,40},{56,48},{64,56},{72,6... | collective-permute-start | bytes 331784 | tf_op jit(solution)/shard_map/ppermute | solution.py:23
  66.7 7.4 %copy-start.4 = (f32[18,40,384]{2,1,0:T(8,128)S(1)}, f32[18,40,384]{2,1,0:T(8,128)}, u32[]{:S(2)}) copy-start(f32[18,40,384]{2,1,0:T(8,128)} %get-tuple-element.20) | copy-start | bytes 3317764
  66.7 7.4 %copy-start.5 = (f32[18,40,384]{2,1,0:T(8,128)S(1)}, f32[18,40,384]{2,1,0:T(8,128)}, u32[]{:S(2)}) copy-start(f32[18,40,384]{2,1,0:T(8,128)} %get-tuple-element.21) | copy-start | bytes 3317764
  66.7 5.0 %collective-permute-start.5 = (f32[4,18,1,384]{3,1,2,0:T(8,128)S(1)}, f32[4,18,1,384]{3,1,2,0:T(8,128)S(1)}, u32[]{:S(2)}, u32[]{:S(2)}) collective-permute-start(f32[4,18,1,384]{3,1,2,0:T(8,128)S(1)} %copy.35), channel_id=1, source_target_pairs={{0,8},{8,16},{16,24},{24,32},{32,40},{40,48},{48,56},{56,64},{64,7... | collective-permute-start | bytes 331784 | tf_op jit(solution)/shard_map/ppermute | solution.py:22
  79.9 2.1 copy-start.3
  82.0 4.4 %copy-start.8 = (f32[4,40,384]{2,1,0:T(8,128)S(1)}, f32[4,40,384]{2,1,0:T(8,128)}, u32[]{:S(2)}) copy-start(f32[4,40,384]{2,1,0:T(8,128)} %param.16) | copy-start | bytes 737284
  82.0 46.7 %copy-start.9 = (s32[32,480]{1,0:T(8,128)S(1)}, s32[32,480]{1,0:T(8,128)}, u32[]{:S(2)}) copy-start(s32[32,480]{1,0:T(8,128)} %param.17) | copy-start | bytes 184324
  113.9 24.8 %all-to-all-start = ((f32[32,1,480]{2,1,0:T(1,128)}), f32[32,1,480]{2,1,0:T(1,128)S(1)}, u32[]{:S(2)}, u32[]{:S(2)}) async-start(f32[32,1,480]{2,1,0:T(1,128)} %psum.7), calls=%async_computation | async-start | bytes 131072 | tf_op jit(solution)/shard_map/all_to_all | solution.py:94
where the time goes:
time: 220 us
  other arithmetic  115 us (52%)
  starting transfers between devices  31.1 us (14%)
  blocking collectives  27.3 us (12%)
  local copies, waits for them, and re-layouts  23.3 us (11%)
  waiting for transfers between devices  17.9 us (8%)
  matrix products  4.36 us (2%)
    scatter-add x1, other arithmetic, shards(): jax.ops.segment_sum(received.reshape(-1), flux_cell.reshape(-1), num_segm...  81 us
    psum x1, blocking collectives, shards(): totals = lax.psum(columns, ('lev', 'sec'))  27.3 us
    all_to_all x1, starting transfers between devices, shards(): lax.all_to_all(totals, 'tile', split_axis=0, concat_axis=0, tiled=True)  14.8 us
    ppermute x2, starting transfers between devices, extended_2(): after = lax.ppermute(initial, axis, down)  13.2 us
    add x2, other arithmetic, sweep_first(): adjoint + ahead * (following - adjoint) + behind * (adjoint - previous)  11.6 us
    all_to_all x1, waiting for transfers between devices, shards(): lax.all_to_all(totals, 'tile', split_axis=0, concat_axis=0, tiled=True)  9.88 us
    slice x2, local copies, waits for them, and re-layouts, sweep_first(): previous = jnp.concatenate([left_rim, adjoint[:, :, :-1]], axis=2)  8.13 us
    add x2, other arithmetic, sweep_second(): adjoint + ahead * (following - adjoint) + behind * (adjoint - previous)  7.2 us
  transfers between devices with their start and end apart: 7, of which 3 were waited for; matrix products, arithmetic and copies ran while one was open for 9% of the time, Pallas kernels for 0%

commit v1 on v0

--- a/solution.py
+++ b/solution.py
@@ -90,7 +90,9 @@
         "sxy,l,slxy->xy", sector_share, level_weight, adjoint, precision=lax.Precision.HIGHEST
     )
     columns = partial_value.reshape(tile_count, -1)
-    totals = lax.psum(columns, ("lev", "sec"))
+    totals = columns
+    for it in ("lev", "sec"):
+        totals = lax.psum(totals, axis_name=it)
     received = lax.all_to_all(totals, "tile", split_axis=0, concat_axis=0, tiled=True)
     flux_sensitivity = jax.ops.segment_sum(
         received.reshape(-1), flux_cell.reshape(-1), num_segments=FL_DEV

time: 220 us -> 212 us (0.964)
  blocking collectives: 27.3 us -> 20.5 us
    psum x1 -> x2, blocking collectives: 27.3 us -> 20.5 us  [shards(): totals = lax.psum(totals, axis_name=it)]
where the time goes in v1:
time: 212 us
  other arithmetic  115 us (54%)
  starting transfers between devices  29.7 us (14%)
  local copies, waits for them, and re-layouts  23.4 us (11%)
  blocking collectives  20.5 us (10%)
  waiting for transfers between devices  18 us (8%)
  matrix products  4.36 us (2%)
    scatter-add x1, other arithmetic, shards(): jax.ops.segment_sum(received.reshape(-1), flux_cell.reshape(-1), num_segm...  81 us
    psum x2, blocking collectives, shards(): totals = lax.psum(totals, axis_name=it)  20.5 us
    all_to_all x1, starting transfers between devices, shards(): lax.all_to_all(totals, 'tile', split_axis=0, concat_axis=0, tiled=True)  13.4 us
    ppermute x2, starting transfers between devices, extended_2(): after = lax.ppermute(initial, axis, down)  13.2 us
    add x2, other arithmetic, sweep_first(): adjoint + ahead * (following - adjoint) + behind * (adjoint - previous)  11.6 us
    all_to_all x1, waiting for transfers between devices, shards(): lax.all_to_all(totals, 'tile', split_axis=0, concat_axis=0, tiled=True)  9.98 us
    slice x2, local copies, waits for them, and re-layouts, sweep_first(): previous = jnp.concatenate([left_rim, adjoint[:, :, :-1]], axis=2)  8.12 us
    add x2, other arithmetic, sweep_second(): adjoint + ahead * (following - adjoint) + behind * (adjoint - previous)  7.2 us
  transfers between devices with their start and end apart: 7, of which 3 were waited for; matrix products, arithmetic and copies ran while one was open for 9% of the time, Pallas kernels for 0%

profile of v1, /device:TPU:1, one launch (start us, length us, event | category | flops | bytes accessed | tf_op | source)
XLA Modules:
  0.0 212.0 jit_solution(988451255206561793)
XLA Ops:
  1.8 1.4 collective-permute-start
  3.2 5.7 %fusion.28 = (f32[18,40,384]{2,1,0:T(8,128)}, f32[18,40,384]{2,1,0:T(8,128)}, f32[18,40,384]{2,1,0:T(8,128)}, f32[18,40,384]{2,1,0:T(8,128)}, f32[18,40,384]{2,1...) fusion(bf16[18,40,384]{2,1,0:T(8,128)(2,1)} %param.10, ...), kind=kLoop, calls=%fused_computation.45 | loop fusion | flops 10506240 | bytes 11059200 | tf_op jit(solution)/shard_map/sub | solution.py:32
  9.0 2.3 %slice.76 = f32[4,17,40,384]{3,2,1,0:T(8,128)} slice(f32[4,18,40,384]{3,2,1,0:T(8,128)S(1)} %bitcast.18), slice={[0:4], [1:18], [0:40], [0:384]} | slice | bytes 8355840 | tf_op jit(solution)/shard_map/slice | solution.py:44
  13.0 4.2 %fusion.3 = f32[4,18,40,384]{3,2,1,0:T(8,128)S(1)} fusion(f32[4,18,40,384]{3,2,1,0:T(8,128)} %param.9, f32[4,1,40,384]{3,2,1,0:T(8,128)S(1)} %slice_select_fusion.1, f32[4,17,40,384]{3,2,1,0:T(8,128)} %slice.76, f32[18,40,384]{2,1,0:T(8,128)S(1)} %convert_element_type.23), kind=kLoop, calls=%fused_computation.5 | loop fusion | flops 4423680 | bytes 14376960 | tf_op jit(solution)/shard_map/add | solution.py:45
  17.2 1.6 fusion.46
  20.2 3.7 %fusion.6 = f32[4,18,40,384]{3,2,1,0:T(8,128)S(1)} fusion(f32[4,18,40,384]{3,2,1,0:T(8,128)S(1)} %fusion.3, f32[4,18,40,1]{3,2,1,0:T(8,128)} %get-tuple-element.17, f32[4,18,40,383]{3,2,1,0:T(8,128)S(1)} %get-tuple-element.19, f32[4,18,40,383]{3,2,1,0:T(8,128)S(1)} %get-tuple-element.18, f32[4,18,40,1]{3,2,1,0:T(8,128)S(1)} %get-tuple-element.16, ...), kind=kLoop, calls=%fused_computation.9 | loop fusion | flops 8847360 | bytes 19906560 | tf_op jit(solution)/shard_map/add | solution.py:52
  24.1 3.3 %collective-permute-start.1 = (f32[4,18,1,384]{3,1,2,0:T(8,128)S(1)}, f32[4,18,1,384]{3,1,2,0:T(8,128)S(1)}, u32[]{:S(2)}, u32[]{:S(2)}) collective-permute-start(f32[4,18,1,384]{3,1,2,0:T(8,128)S(1)} %copy.26), channel_id=1, source_target_pairs={{8,0},{16,8},{24,16},{32,24},{40,32},{48,40},{56,48},{64,56},{72,6... | collective-permute-start | bytes 331784 | tf_op jit(solution)/shard_map/ppermute | solution.py:23
  27.6 4.1 %fusion.45 = (f32[4,18,39,384]{3,2,1,0:T(8,128)}, f32[4,18,39,384]{3,2,1,0:T(8,128)}) fusion(f32[4,18,40,384]{3,2,1,0:T(8,128)S(1)} %fusion.6), kind=kLoop, calls=%fused_computation.74 | loop fusion | bytes 17252352 | tf_op jit(solution)/shard_map/slice | solution.py:61
  32.5 2.2 %collective-permute-done.2 = f32[4,18,1,384]{3,1,2,0:T(8,128)S(1)} collective-permute-done((f32[4,18,1,384]{3,1,2,0:T(8,128)S(1)}, f32[4,18,1,384]{3,1,2,0:T(8,128)S(1)}, u32[]{:S(2)}, u32[]{:S(2)}) %collective-permute-start.2) | collective-permute-done | bytes 110624 | tf_op jit(solution)/shard_map/ppermute | solution.py:22
  37.1 5.9 %fusion.10 = f32[4,18,40,384]{3,2,1,0:T(8,128)S(1)} fusion(f32[4,18,40,384]{3,2,1,0:T(8,128)} %copy-done.2, f32[4,18,1,384]{3,2,1,0:T(1,128)S(1)} %broadcast_select_fusion.3, f32[4,18,39,384]{3,2,1,0:T(8,128)} %get-tuple-element.15, f32[4,18,39,384]{3,2,1,0:T(8,128)} %get-tuple-element.14, f32[4,18,1,384]{3,2,1,0:T(1,128)S(1)} %broadcast_select_fusion.1, ...), kind=kLoop, calls=%fused_computation.15 | loop fusion | flops 8847360 | bytes 19906560 | tf_op jit(solution)/shard_map/add | solution.py:62
  43.1 1.5 collective-permute-start.3
  44.8 5.8 %collective-permute-done.3 = f32[4,1,40,384]{3,2,1,0:T(8,128)S(1)} collective-permute-done((f32[4,1,40,384]{3,2,1,0:T(8,128)S(1)}, f32[4,1,40,384]{3,2,1,0:T(8,128)S(1)}, u32[]{:S(2)}, u32[]{:S(2)}) %collective-permute-start.3) | collective-permute-done | bytes 245792 | tf_op jit(solution)/shard_map/ppermute | solution.py:12
  51.8 1.4 fusion.43
  53.2 3.5 %fusion.16 = f32[4,18,40,384]{3,2,1,0:T(8,128)S(1)} fusion(f32[4,18,40,384]{3,2,1,0:T(8,128)S(1)} %fusion.13, f32[4,18,40,1]{3,2,1,0:T(8,128)S(1)} %get-tuple-element.9, f32[4,18,40,383]{3,2,1,0:T(8,128)S(1)} %get-tuple-element.11, f32[4,18,40,383]{3,2,1,0:T(8,128)S(1)} %get-tuple-element.10, f32[4,18,40,1]{3,2,1,0:T(8,128)S(1)} %get-tuple-element.8, ...), kind=kLoop, calls=%fused_computation.24 | loop fusion | flops 8847360 | bytes 19906560 | tf_op jit(solution)/shard_map/add | solution.py:52
  56.9 9.9 %collective-permute-start.4 = (f32[4,18,1,384]{3,1,2,0:T(8,128)S(1)}, f32[4,18,1,384]{3,1,2,0:T(8,128)S(1)}, u32[]{:S(2)}, u32[]{:S(2)}) collective-permute-start(f32[4,18,1,384]{3,1,2,0:T(8,128)S(1)} %copy.32), channel_id=1, source_target_pairs={{8,0},{16,8},{24,16},{32,24},{40,32},{48,40},{56,48},{64,56},{72,6... | collective-permute-start | bytes 331784 | tf_op jit(solution)/shard_map/ppermute | solution.py:23
  67.0 4.1 %fusion.41 = (f32[4,18,39,384]{3,2,1,0:T(8,128)}, f32[4,18,39,384]{3,2,1,0:T(8,128)}) fusion(f32[4,18,40,384]{3,2,1,0:T(8,128)S(1)} %fusion.16), kind=kLoop, calls=%fused_computation.70 | loop fusion | bytes 17252352 | tf_op jit(solution)/shard_map/slice | solution.py:61
  74.4 5.7 %fusion.20 = f32[4,18,40,384]{3,2,1,0:T(8,128)S(1)} fusion(f32[4,18,40,384]{3,2,1,0:T(8,128)} %copy-done.1, f32[4,18,1,384]{3,2,1,0:T(1,128)S(1)} %broadcast_select_fusion.2, f32[4,18,39,384]{3,2,1,0:T(8,128)} %get-tuple-element.7, f32[4,18,39,384]{3,2,1,0:T(8,128)} %get-tuple-element.6, f32[4,18,1,384]{3,2,1,0:T(1,128)S(1)} %broadcast_select_fusion, ...), kind=kLoop, calls=%fused_computation.30 | loop fusion | flops 8847360 | bytes 19906560 | tf_op jit(solution)/shard_map/add | solution.py:62
  80.1 2.1 copy-done.3
  82.2 4.4 %fusion = f32[1,4,40,384]{3,0,2,1:T(1,128)S(1)} fusion(f32[4,18,40,384]{3,2,1,0:T(8,128)S(1)} %fusion.20, f32[18]{0:T(128)S(1)} %copy-done), kind=kOutput, calls=%fused_computation.1 | convolution fusion | flops 13271040 | bytes 4669512 | tf_op jit(solution)/shard_map/sxy,l,slxy->xy/dot_general | solution.py:89
  86.7 13.0 %psum.14 = f32[32,480]{1,0:T(8,128)S(1)} all-reduce(f32[32,480]{1,0:T(8,128)S(1)} %reshape.28), channel_id=1, replica_groups=mesh['tile'=32,'lev'=4,'sec'=2] {'lev'}, use_global_device_ids=true, to_apply=%region_0.1 | all-reduce | flops 15360 | bytes 122880 | tf_op jit(solution)/shard_map/psum | solution.py:95
  99.8 7.5 %psum.15 = f32[32,1,480]{2,1,0:T(1,128)} all-reduce(f32[32,1,480]{2,1,0:T(1,128)S(1)} %all_to_all.6), channel_id=1, replica_groups=mesh['tile'=32,'lev'=4,'sec'=2] {'sec'}, use_global_device_ids=true, to_apply=%region_1.2 | all-reduce | flops 15360 | bytes 122880 | tf_op jit(solution)/shard_map/psum | solution.py:95
  107.2 13.4 %all-to-all-start = ((f32[32,1,480]{2,1,0:T(1,128)}), f32[32,1,480]{2,1,0:T(1,128)S(1)}, u32[]{:S(2)}, u32[]{:S(2)}) async-start(f32[32,1,480]{2,1,0:T(1,128)} %psum.15), calls=%async_computation | async-start | bytes 131072 | tf_op jit(solution)/shard_map/all_to_all | solution.py:96
  120.8 10.0 %all-to-all-done = f32[32,1,480]{2,1,0:T(1,128)S(1)} async-done(((f32[32,1,480]{2,1,0:T(1,128)}), f32[32,1,480]{2,1,0:T(1,128)S(1)}, u32[]{:S(2)}, u32[]{:S(2)}) %all-to-all-start) | async-done | bytes 61472 | tf_op jit(solution)/shard_map/all_to_all | solution.py:96
  131.0 81.0 %scatter_custom_fusion = f32[15360]{0:T(1024)} fusion(s32[15360]{0:T(1024)S(1)} %reshape.32, f32[15360]{0:T(1024)S(1)} %reshape.34, f32[]{:T(128)} %constant.16.clone.1), kind=kCustom, calls=%fused_computation.65 | custom fusion | flops 15360 | bytes 61444 | tf_op jit(solution)/shard_map/scatter-add | solution.py:97
  (67 shorter events, 13.4 us)
Async XLA Ops:
  0.6 81.5 %copy-start = (f32[18]{0:T(128)S(1)}, f32[18]{0:T(128)}, u32[]{:S(2)}) copy-start(f32[18]{0:T(128)} %param.15) | copy-start | bytes 220
  0.6 8.3 %slice-start = ((s8[4423680]{0:T(1024)(128)(4,1)}), s8[4194304]{0:T(1024)(128)(4,1)S(1)}, s32[]{:S(2)}) async-start(s8[4423680]{0:T(1024)(128)(4,1)} %bitcast.17), calls=%async_computation.1 | async-start | bytes 8388608
  1.8 7.2 %slice-start.1 = ((s8[4423680]{0:T(1024)(128)(4,1)}), s8[229376]{0:T(1024)(128)(4,1)S(1)}, s32[]{:S(2)}) async-start(s8[4423680]{0:T(1024)(128)(4,1)} %bitcast.17), calls=%async_computation.2 | async-start | bytes 458752
  1.8 10.3 %collective-permute-start = (f32[4,1,40,384]{3,2,1,0:T(8,128)S(1)}, f32[4,1,40,384]{3,2,1,0:T(8,128)S(1)}, u32[]{:S(2)}, u32[]{:S(2)}) collective-permute-start(f32[4,1,40,384]{3,2,1,0:T(8,128)S(1)} %slice.78), channel_id=1, source_target_pairs={{2,0},{4,2},{6,4},{3,1},{5,3},{7,5},{10,8},{12,10},{14,12},{11,9},... | collective-permute-start | bytes 737288 | tf_op jit(solution)/shard_map/ppermute | solution.py:12
  9.0 2.3 %copy-start.7 = (bf16[18,40,384]{2,1,0:T(8,128)(2,1)S(1)}, bf16[18,40,384]{2,1,0:T(8,128)(2,1)}, u32[]{:S(2)}) copy-start(bf16[18,40,384]{2,1,0:T(8,128)(2,1)} %param.12) | copy-start | bytes 1658884
  9.0 2.4 %copy-start.10 = (s32[32,2]{0,1:T(2,128)S(1)}, s32[32,2]{0,1:T(2,128)}, u32[]{:S(2)}) copy-start(s32[32,2]{0,1:T(2,128)} %param.14) | copy-start | bytes 772
  23.9 7.7 %copy-start.2 = (f32[4,18,40,384]{3,2,1,0:T(8,128)}, f32[4,18,40,384]{3,2,1,0:T(8,128)S(1)}, u32[]{:S(2)}) copy-start(f32[4,18,40,384]{3,2,1,0:T(8,128)S(1)} %fusion.6) | copy-start | bytes 13271044
  24.1 7.5 %collective-permute-start.1 = (f32[4,18,1,384]{3,1,2,0:T(8,128)S(1)}, f32[4,18,1,384]{3,1,2,0:T(8,128)S(1)}, u32[]{:S(2)}, u32[]{:S(2)}) collective-permute-start(f32[4,18,1,384]{3,1,2,0:T(8,128)S(1)} %copy.26), channel_id=1, source_target_pairs={{8,0},{16,8},{24,16},{32,24},{40,32},{48,40},{56,48},{64,56},{72,6... | collective-permute-start | bytes 331784 | tf_op jit(solution)/shard_map/ppermute | solution.py:23
  27.5 9.6 %copy-start.6 = (f32[18,40,384]{2,1,0:T(8,128)S(1)}, f32[18,40,384]{2,1,0:T(8,128)}, u32[]{:S(2)}) copy-start(f32[18,40,384]{2,1,0:T(8,128)} %get-tuple-element.22) | copy-start | bytes 3317764
  27.5 7.1 %collective-permute-start.2 = (f32[4,18,1,384]{3,1,2,0:T(8,128)S(1)}, f32[4,18,1,384]{3,1,2,0:T(8,128)S(1)}, u32[]{:S(2)}, u32[]{:S(2)}) collective-permute-start(f32[4,18,1,384]{3,1,2,0:T(8,128)S(1)} %copy.29), channel_id=1, source_target_pairs={{0,8},{8,16},{16,24},{24,32},{32,40},{40,48},{48,56},{56,64},{64,7... | collective-permute-start | bytes 331784 | tf_op jit(solution)/shard_map/ppermute | solution.py:22
  43.1 7.6 %collective-permute-start.3 = (f32[4,1,40,384]{3,2,1,0:T(8,128)S(1)}, f32[4,1,40,384]{3,2,1,0:T(8,128)S(1)}, u32[]{:S(2)}, u32[]{:S(2)}) collective-permute-start(f32[4,1,40,384]{3,2,1,0:T(8,128)S(1)} %slice.110), channel_id=1, source_target_pairs={{2,0},{4,2},{6,4},{3,1},{5,3},{7,5},{10,8},{12,10},{14,12},{11,9},... | collective-permute-start | bytes 737288 | tf_op jit(solution)/shard_map/ppermute | solution.py:12
  56.7 14.3 %copy-start.1 = (f32[4,18,40,384]{3,2,1,0:T(8,128)}, f32[4,18,40,384]{3,2,1,0:T(8,128)S(1)}, u32[]{:S(2)}) copy-start(f32[4,18,40,384]{3,2,1,0:T(8,128)S(1)} %fusion.16) | copy-start | bytes 13271044
  56.9 14.1 %collective-permute-start.4 = (f32[4,18,1,384]{3,1,2,0:T(8,128)S(1)}, f32[4,18,1,384]{3,1,2,0:T(8,128)S(1)}, u32[]{:S(2)}, u32[]{:S(2)}) collective-permute-start(f32[4,18,1,384]{3,1,2,0:T(8,128)S(1)} %copy.32), channel_id=1, source_target_pairs={{8,0},{16,8},{24,16},{32,24},{40,32},{48,40},{56,48},{64,56},{72,6... | collective-permute-start | bytes 331784 | tf_op jit(solution)/shard_map/ppermute | solution.py:23
  66.9 7.5 %copy-start.4 = (f32[18,40,384]{2,1,0:T(8,128)S(1)}, f32[18,40,384]{2,1,0:T(8,128)}, u32[]{:S(2)}) copy-start(f32[18,40,384]{2,1,0:T(8,128)} %get-tuple-element.20) | copy-start | bytes 3317764
  66.9 7.5 %copy-start.5 = (f32[18,40,384]{2,1,0:T(8,128)S(1)}, f32[18,40,384]{2,1,0:T(8,128)}, u32[]{:S(2)}) copy-start(f32[18,40,384]{2,1,0:T(8,128)} %get-tuple-element.21) | copy-start | bytes 3317764
  66.9 5.0 %collective-permute-start.5 = (f32[4,18,1,384]{3,1,2,0:T(8,128)S(1)}, f32[4,18,1,384]{3,1,2,0:T(8,128)S(1)}, u32[]{:S(2)}, u32[]{:S(2)}) collective-permute-start(f32[4,18,1,384]{3,1,2,0:T(8,128)S(1)} %copy.35), channel_id=1, source_target_pairs={{0,8},{8,16},{16,24},{24,32},{32,40},{40,48},{48,56},{56,64},{64,7... | collective-permute-start | bytes 331784 | tf_op jit(solution)/shard_map/ppermute | solution.py:22
  80.1 2.1 copy-start.3
  82.2 4.4 %copy-start.8 = (f32[4,40,384]{2,1,0:T(8,128)S(1)}, f32[4,40,384]{2,1,0:T(8,128)}, u32[]{:S(2)}) copy-start(f32[4,40,384]{2,1,0:T(8,128)} %param.16) | copy-start | bytes 737284
  82.2 38.5 %copy-start.9 = (s32[32,480]{1,0:T(8,128)S(1)}, s32[32,480]{1,0:T(8,128)}, u32[]{:S(2)}) copy-start(s32[32,480]{1,0:T(8,128)} %param.17) | copy-start | bytes 184324
  107.2 23.5 %all-to-all-start = ((f32[32,1,480]{2,1,0:T(1,128)}), f32[32,1,480]{2,1,0:T(1,128)S(1)}, u32[]{:S(2)}, u32[]{:S(2)}) async-start(f32[32,1,480]{2,1,0:T(1,128)} %psum.15), calls=%async_computation | async-start | bytes 131072 | tf_op jit(solution)/shard_map/all_to_all | solution.py:96
